TPU v7x, 1024 devices: a whole 8x8x8 slice. The times are simulated.
1024 devices in a mesh: grp: 4 (over y_lo), slab: 8 (over x), brick: 32 (over z, y_hi, core).
Axes of the slice: x: 8, y: 8 (y_hi: 2, y_lo: 4; y = y_hi * 4 + y_lo), z: 8, core: 2. Of those that a mesh axis runs over, the one named last changes fastest.
Arguments:
- voxel_warmth: float32 [128, 64, 8192], P('slab', 'grp', 'brick'), may hold values from -6 to 6
- consolidated_flag: int32 [128, 64, 8192], P('slab', 'grp', 'brick'), may hold values 0 or 1
- beam_north_position: int32 [2, 4], replicated, may hold values from 0 to 63
- beam_east_position: int32 [2, 4], replicated, may hold values from 0 to 8191
Outputs:
- warmth_after_substep: float32 [128, 64, 8192], P('slab', 'grp', 'brick')
- coarse_shift_vector: float32 [3, 64, 32, 4096], P(None, 'slab', 'grp', 'brick')
All inputs are finite; a program needn't handle non-finite values. No bound on the sum of `consolidated_flag` on one device may be relied on, other than what follows from the above.
Results may differ from a plain program's by a relative error of at most 0.0001.
Values sent between devices are 32-bit elements; how exact they have to be, the bound alone decides.
A program may use at most 64 MiB of HBM per device.

v0:
```python
import jax
import jax.numpy as jnp
from jax import lax
from jax.sharding import PartitionSpec as P

SUBSTEPS = 2
SWEEPS = 6


time_step = 0.15
spot_power = 30.0
solid_kappa = 1.0
powder_kappa = 0.2
shear_modulus = 1.0
coupling = 1.5
stress_factor = 8.0
eigen_low = 0.5
eigen_high = 3.5


def padded_2(array, sides, width):
    for axis, dim in sides:
        size, length = (lax.axis_size(axis), array.shape[dim])
        up = [(i, (i + 1) % size) for i in range(size - 1)]
        down = [(j, i) for i, j in up]
        last = lax.slice_in_dim(array, length - width, length, axis=dim)
        initial = lax.slice_in_dim(array, 0, width, axis=dim)
        before = lax.ppermute(last, axis, up)
        after = lax.ppermute(initial, axis, down)
        array = jnp.concatenate([before, array, after], axis=dim)
    return array


def neighbour(padded, axis_pick, forward):
    pieces = []
    for axis_number in range(3):
        if axis_number == axis_pick:
            pieces.append(slice(2, None) if forward else slice(0, -2))
        else:
            pieces.append(slice(1, -1))
    return padded[tuple(pieces)]


def thermal_advance(bordered_warmth, bordered_diffusivity, injected_power):
    centre_heat = bordered_warmth[1:-1, 1:-1, 1:-1]
    centre_kappa = bordered_diffusivity[1:-1, 1:-1, 1:-1]
    total = jnp.zeros_like(centre_heat)
    for axis_pick in range(3):
        for forward in (True, False):
            other_kappa = neighbour(bordered_diffusivity, axis_pick, forward)
            other_heat = neighbour(bordered_warmth, axis_pick, forward)
            face = 2.0 * centre_kappa * other_kappa / (centre_kappa + other_kappa)
            total = total + face * (other_heat - centre_heat)
    capacity = 0.375 + 0.625 * centre_kappa
    return centre_heat + time_step * (total + injected_power) / capacity


def laser_source(row_y, row_x, start_z, start_y, start_x, shape_zyx, top_layer):
    vertical_span, count_across_north, count_across_east = shape_zyx
    zpos = start_z + jnp.arange(vertical_span, dtype=jnp.int32)
    ypos = start_y + jnp.arange(count_across_north, dtype=jnp.int32)
    xpos = start_x + jnp.arange(count_across_east, dtype=jnp.int32)
    hit_rows = (ypos[None, :] == row_y[:, None]).astype(jnp.float32)
    hit_columns = (xpos[None, :] == row_x[:, None]).astype(jnp.float32)
    plane = jnp.dot(
        hit_rows.T, hit_columns, precision=lax.Precision.HIGHEST, preferred_element_type=jnp.float32
    )
    layer = (zpos == top_layer - 1).astype(jnp.float32)
    return spot_power * layer[:, None, None] * plane[None, :, :]


def kappa_from(consolidated_flag):
    return powder_kappa + (solid_kappa - powder_kappa) * consolidated_flag.astype(jnp.float32)


def merge_blocks(field):
    vertical_span, count_across_north, count_across_east = field.shape
    blocks = field.reshape(
        vertical_span // 2, 2, count_across_north // 2, 2, count_across_east // 2, 2
    )
    return jnp.sum(blocks, axis=(1, 3, 5)) * 0.125


def thermal_force(padded):
    half = 0.5 * stress_factor
    return jnp.stack(
        [
            half * (padded[:-2, 1:-1, 1:-1] - padded[2:, 1:-1, 1:-1]),
            half * (padded[1:-1, :-2, 1:-1] - padded[1:-1, 2:, 1:-1]),
            half * (padded[1:-1, 1:-1, :-2] - padded[1:-1, 1:-1, 2:]),
        ]
    )


def apply_operator(padded, spring):
    centre = padded[:, 1:-1, 1:-1, 1:-1]
    neighbours = (
        padded[:, 2:, 1:-1, 1:-1]
        + padded[:, :-2, 1:-1, 1:-1]
        + padded[:, 1:-1, 2:, 1:-1]
        + padded[:, 1:-1, :-2, 1:-1]
        + padded[:, 1:-1, 1:-1, 2:]
        + padded[:, 1:-1, 1:-1, :-2]
    )
    divergence = (
        padded[0, 1:, :-1, :-1]
        - padded[0, :-1, :-1, :-1]
        + (padded[1, :-1, 1:, :-1] - padded[1, :-1, :-1, :-1])
        + (padded[2, :-1, :-1, 1:] - padded[2, :-1, :-1, :-1])
    )
    inner = divergence[1:, 1:, 1:]
    backward = jnp.stack(
        [
            divergence[:-1, 1:, 1:] - inner,
            divergence[1:, :-1, 1:] - inner,
            divergence[1:, 1:, :-1] - inner,
        ]
    )
    return shear_modulus * (6.0 * centre - neighbours) + coupling * backward + spring * centre


def motion_rim(direction):
    return padded_2(direction, (("grp", 2), ("slab", 1), ("brick", 3)), 1)


def per_device(voxel_warmth, consolidated_flag, beam_north_position, beam_east_position):
    vertical_span, count_across_north, count_across_east = voxel_warmth.shape
    totals = (
        vertical_span * lax.axis_size("slab"),
        count_across_north * lax.axis_size("grp"),
        count_across_east * lax.axis_size("brick"),
    )
    start_z = lax.axis_index("slab") * vertical_span
    start_y = lax.axis_index("grp") * count_across_north
    start_x = lax.axis_index("brick") * count_across_east
    kappa = kappa_from(consolidated_flag)
    bordered_diffusivity = padded_2(kappa, (("grp", 1), ("slab", 0), ("brick", 2)), 1)
    warmth_after_substep = voxel_warmth
    for substep in range(SUBSTEPS):
        bordered_warmth = padded_2(warmth_after_substep, (("grp", 1), ("slab", 0), ("brick", 2)), 1)
        injected_power = laser_source(
            beam_north_position[substep],
            beam_east_position[substep],
            start_z,
            start_y,
            start_x,
            (vertical_span, count_across_north, count_across_east),
            totals[0],
        )
        warmth_after_substep = thermal_advance(
            bordered_warmth, bordered_diffusivity, injected_power
        )
    dense_material_flag = consolidated_flag.astype(jnp.float32)
    deformation_gradient = merge_blocks(dense_material_flag * warmth_after_substep)
    spring = 0.5 + 1.5 * merge_blocks(dense_material_flag)
    centre_value = (eigen_high + eigen_low) / 2.0
    radius = (eigen_high - eigen_low) / 2.0
    sigma_ratio = centre_value / radius
    rho_prev = 1.0 / sigma_ratio
    padded_strain = padded_2(deformation_gradient, (("grp", 1), ("slab", 0), ("brick", 2)), 1)
    force = thermal_force(padded_strain)
    diagonal = 6.0 * shear_modulus + 2.0 * coupling + spring
    coarse_shift_vector = jnp.zeros_like(force)
    residual = force
    direction = residual / diagonal * (1.0 / centre_value)
    for sweep_index in range(SWEEPS):
        coarse_shift_vector = coarse_shift_vector + direction
        if sweep_index + 1 < SWEEPS:
            padded = motion_rim(direction)
            residual = residual - apply_operator(padded, spring)
            rho_next = 1.0 / (2.0 * sigma_ratio - rho_prev)
            direction = rho_next * rho_prev * direction + 2.0 * rho_next / radius * (
                residual / diagonal
            )
            rho_prev = rho_next
    return (warmth_after_substep, coarse_shift_vector)


def solution(mesh):
    in_specs = (P("slab", "grp", "brick"), P("slab", "grp", "brick"), P(), P())
    out_specs = (P("slab", "grp", "brick"), P(None, "slab", "grp", "brick"))
    return jax.shard_map(
        per_device, mesh=mesh, in_specs=in_specs, out_specs=out_specs, check_vma=False
    )
```

profile of v0, /device:TPU:493, one launch (start us, length us, event | category | flops | bytes accessed | tf_op | source)
XLA Modules:
  0.0 379.4 jit_solution(16229700250946775859)
XLA Ops:
  25.9 9.8 %collective-permute-start.10 = (f32[18,18,1]{2,1,0:T(8,128)S(1)}, f32[18,18,1]{2,1,0:T(8,128)S(1)}, u32[]{:S(2)}, u32[]{:S(2)}) collective-permute-start(f32[18,18,1]{2,1,0:T(8,128)S(1)} %get-tuple-element.14), channel_id=1, source_target_pairs={{0,1},{1,2},{2,3},{3,4},{4,5},{5,6},{6,7},{7,8},{8,9},{9,10},{10,1... | collective-permute-start | bytes 3896 | tf_op jit(solution)/shard_map/ppermute | solution.py:28
  38.8 9.7 %collective-permute-start.11 = (f32[18,18,1]{2,1,0:T(8,128)S(1)}, f32[18,18,1]{2,1,0:T(8,128)S(1)}, u32[]{:S(2)}, u32[]{:S(2)}) collective-permute-start(f32[18,18,1]{2,1,0:T(8,128)S(1)} %get-tuple-element.17), channel_id=1, source_target_pairs={{0,1},{1,2},{2,3},{3,4},{4,5},{5,6},{6,7},{7,8},{8,9},{9,10},{10,1... | collective-permute-start | bytes 3896 | tf_op jit(solution)/shard_map/ppermute | solution.py:28
  57.9 5.6 %collective-permute-done.9 = f32[18,18,1]{2,1,0:T(8,128)S(1)} collective-permute-done((f32[18,18,1]{2,1,0:T(8,128)S(1)}, f32[18,18,1]{2,1,0:T(8,128)S(1)}, u32[]{:S(2)}, u32[]{:S(2)}) %collective-permute-start.9) | collective-permute-done | bytes 1328 | tf_op jit(solution)/shard_map/ppermute | solution.py:29
  82.5 9.7 %collective-permute-start.17 = (f32[18,18,1]{2,1,0:T(8,128)S(1)}, f32[18,18,1]{2,1,0:T(8,128)S(1)}, u32[]{:S(2)}, u32[]{:S(2)}) collective-permute-start(f32[18,18,1]{2,1,0:T(8,128)S(1)} %get-tuple-element.13), channel_id=1, source_target_pairs={{0,1},{1,2},{2,3},{3,4},{4,5},{5,6},{6,7},{7,8},{8,9},{9,10},{10,1... | collective-permute-start | bytes 3896 | tf_op jit(solution)/shard_map/ppermute | solution.py:28
  92.4 7.6 %collective-permute-done.16 = f32[18,18,1]{2,1,0:T(8,128)S(1)} collective-permute-done((f32[18,18,1]{2,1,0:T(8,128)S(1)}, f32[18,18,1]{2,1,0:T(8,128)S(1)}, u32[]{:S(2)}, u32[]{:S(2)}) %collective-permute-start.16) | collective-permute-done | bytes 1328 | tf_op jit(solution)/shard_map/ppermute | solution.py:29
  102.5 18.1 %reshape.63 = f32[8,2,8,2,128,2]{5,4,3,2,1,0:T(8,128)} reshape(f32[16,16,256]{2,1,0:T(8,128)S(1)} %get-tuple-element.10) | data formatting | bytes 524288 | tf_op jit(solution)/shard_map/reshape | solution.py:78
  120.6 7.0 %reduce_sum.18 = f32[8,8,128]{2,1,0:T(8,128)S(1)} reduce(f32[8,2,8,2,128,2]{5,4,3,2,1,0:T(8,128)} %reshape.63, f32[]{:T(128)} %constant.18.clone.1), dimensions={1,3,5}, to_apply=%region_0.0 | reduce | flops 57344 | bytes 294916 | tf_op jit(solution)/shard_map/reduce_sum | solution.py:81
  133.6 18.1 %reshape.64 = f32[8,2,8,2,128,2]{5,4,3,2,1,0:T(8,128)} reshape(f32[16,16,256]{2,1,0:T(8,128)S(1)} %convert_element_type.3) | data formatting | bytes 524288 | tf_op jit(solution)/shard_map/reshape | solution.py:78
  151.7 7.0 %reduce_sum.19 = f32[8,8,128]{2,1,0:T(8,128)S(1)} reduce(f32[8,2,8,2,128,2]{5,4,3,2,1,0:T(8,128)} %reshape.64, f32[]{:T(128)} %constant.18.clone.1), dimensions={1,3,5}, to_apply=%region_1.0 | reduce | flops 57344 | bytes 294916 | tf_op jit(solution)/shard_map/reduce_sum | solution.py:81
  165.8 8.8 %collective-permute-start.22 = (f32[10,10,1]{2,1,0:T(8,128)S(1)}, f32[10,10,1]{2,1,0:T(8,128)S(1)}, u32[]{:S(2)}, u32[]{:S(2)}) collective-permute-start(f32[10,10,1]{2,1,0:T(8,128)S(1)} %get-tuple-element.75), channel_id=1, source_target_pairs={{0,1},{1,2},{2,3},{3,4},{4,5},{5,6},{6,7},{7,8},{8,9},{9,10},{10,1... | collective-permute-start | bytes 1208 | tf_op jit(solution)/shard_map/ppermute | solution.py:28
  177.7 9.5 %collective-permute-done.23 = f32[10,10,1]{2,1,0:T(8,128)S(1)} collective-permute-done((f32[10,10,1]{2,1,0:T(8,128)S(1)}, f32[10,10,1]{2,1,0:T(8,128)S(1)}, u32[]{:S(2)}, u32[]{:S(2)}) %collective-permute-start.23) | collective-permute-done | bytes 432 | tf_op jit(solution)/shard_map/ppermute | solution.py:29
  210.3 8.5 %collective-permute-done.29 = f32[3,10,10,1]{3,2,1,0:T(8,128)S(1)} collective-permute-done((f32[3,10,10,1]{3,2,1,0:T(8,128)S(1)}, f32[3,10,10,1]{3,2,1,0:T(8,128)S(1)}, u32[]{:S(2)}, u32[]{:S(2)}) %collective-permute-start.29) | collective-permute-done | bytes 1232 | tf_op jit(solution)/shard_map/ppermute | solution.py:28
  219.1 5.4 %collective-permute-done.28 = f32[3,10,10,1]{3,2,1,0:T(8,128)S(1)} collective-permute-done((f32[3,10,10,1]{3,2,1,0:T(8,128)S(1)}, f32[3,10,10,1]{3,2,1,0:T(8,128)S(1)}, u32[]{:S(2)}, u32[]{:S(2)}) %collective-permute-start.28) | collective-permute-done | bytes 1232 | tf_op jit(solution)/shard_map/ppermute | solution.py:29
  231.3 5.1 %collective-permute-start.32 = (f32[3,1,10,128]{3,2,1,0:T(8,128)S(1)}, f32[3,1,10,128]{3,2,1,0:T(8,128)S(1)}, u32[]{:S(2)}, u32[]{:S(2)}) collective-permute-start(f32[3,1,10,128]{3,2,1,0:T(8,128)S(1)} %get-tuple-element.62), channel_id=1, source_target_pairs={{32,0},{64,32},{96,64},{128,96},{160,128},{192,160},{224,192},{33,... | collective-permute-start | bytes 46088 | tf_op jit(solution)/shard_map/ppermute | solution.py:29
  242.7 7.7 %collective-permute-start.35 = (f32[3,10,10,1]{3,2,1,0:T(8,128)S(1)}, f32[3,10,10,1]{3,2,1,0:T(8,128)S(1)}, u32[]{:S(2)}, u32[]{:S(2)}) collective-permute-start(f32[3,10,10,1]{3,2,1,0:T(8,128)S(1)} %get-tuple-element.37), channel_id=1, source_target_pairs={{0,1},{1,2},{2,3},{3,4},{4,5},{5,6},{6,7},{7,8},{8,9},{9,10},{10,1... | collective-permute-start | bytes 3608 | tf_op jit(solution)/shard_map/ppermute | solution.py:28
  252.3 6.0 %collective-permute-done.35 = f32[3,10,10,1]{3,2,1,0:T(8,128)S(1)} collective-permute-done((f32[3,10,10,1]{3,2,1,0:T(8,128)S(1)}, f32[3,10,10,1]{3,2,1,0:T(8,128)S(1)}, u32[]{:S(2)}, u32[]{:S(2)}) %collective-permute-start.35) | collective-permute-done | bytes 1232 | tf_op jit(solution)/shard_map/ppermute | solution.py:28
  258.6 8.1 %collective-permute-done.34 = f32[3,10,10,1]{3,2,1,0:T(8,128)S(1)} collective-permute-done((f32[3,10,10,1]{3,2,1,0:T(8,128)S(1)}, f32[3,10,10,1]{3,2,1,0:T(8,128)S(1)}, u32[]{:S(2)}, u32[]{:S(2)}) %collective-permute-start.34) | collective-permute-done | bytes 1232 | tf_op jit(solution)/shard_map/ppermute | solution.py:29
  282.0 7.0 %collective-permute-start.41 = (f32[3,10,10,1]{3,2,1,0:T(8,128)S(1)}, f32[3,10,10,1]{3,2,1,0:T(8,128)S(1)}, u32[]{:S(2)}, u32[]{:S(2)}) collective-permute-start(f32[3,10,10,1]{3,2,1,0:T(8,128)S(1)} %get-tuple-element.35), channel_id=1, source_target_pairs={{0,1},{1,2},{2,3},{3,4},{4,5},{5,6},{6,7},{7,8},{8,9},{9,10},{10,1... | collective-permute-start | bytes 3608 | tf_op jit(solution)/shard_map/ppermute | solution.py:28
  291.0 5.3 %collective-permute-done.41 = f32[3,10,10,1]{3,2,1,0:T(8,128)S(1)} collective-permute-done((f32[3,10,10,1]{3,2,1,0:T(8,128)S(1)}, f32[3,10,10,1]{3,2,1,0:T(8,128)S(1)}, u32[]{:S(2)}, u32[]{:S(2)}) %collective-permute-start.41) | collective-permute-done | bytes 1232 | tf_op jit(solution)/shard_map/ppermute | solution.py:28
  296.5 8.3 %collective-permute-done.40 = f32[3,10,10,1]{3,2,1,0:T(8,128)S(1)} collective-permute-done((f32[3,10,10,1]{3,2,1,0:T(8,128)S(1)}, f32[3,10,10,1]{3,2,1,0:T(8,128)S(1)}, u32[]{:S(2)}, u32[]{:S(2)}) %collective-permute-start.40) | collective-permute-done | bytes 1232 | tf_op jit(solution)/shard_map/ppermute | solution.py:29
  319.2 6.6 %collective-permute-start.47 = (f32[3,10,10,1]{3,2,1,0:T(8,128)S(1)}, f32[3,10,10,1]{3,2,1,0:T(8,128)S(1)}, u32[]{:S(2)}, u32[]{:S(2)}) collective-permute-start(f32[3,10,10,1]{3,2,1,0:T(8,128)S(1)} %get-tuple-element.33), channel_id=1, source_target_pairs={{0,1},{1,2},{2,3},{3,4},{4,5},{5,6},{6,7},{7,8},{8,9},{9,10},{10,1... | collective-permute-start | bytes 3608 | tf_op jit(solution)/shard_map/ppermute | solution.py:28
  332.4 6.9 %collective-permute-done.46 = f32[3,10,10,1]{3,2,1,0:T(8,128)S(1)} collective-permute-done((f32[3,10,10,1]{3,2,1,0:T(8,128)S(1)}, f32[3,10,10,1]{3,2,1,0:T(8,128)S(1)}, u32[]{:S(2)}, u32[]{:S(2)}) %collective-permute-start.46) | collective-permute-done | bytes 1232 | tf_op jit(solution)/shard_map/ppermute | solution.py:29
  355.0 7.1 %collective-permute-start.53 = (f32[3,10,10,1]{3,2,1,0:T(8,128)S(1)}, f32[3,10,10,1]{3,2,1,0:T(8,128)S(1)}, u32[]{:S(2)}, u32[]{:S(2)}) collective-permute-start(f32[3,10,10,1]{3,2,1,0:T(8,128)S(1)} %get-tuple-element.31), channel_id=1, source_target_pairs={{0,1},{1,2},{2,3},{3,4},{4,5},{5,6},{6,7},{7,8},{8,9},{9,10},{10,1... | collective-permute-start | bytes 3608 | tf_op jit(solution)/shard_map/ppermute | solution.py:28
  368.1 10.3 %collective-permute-done.52 = f32[3,10,10,1]{3,2,1,0:T(8,128)S(1)} collective-permute-done((f32[3,10,10,1]{3,2,1,0:T(8,128)S(1)}, f32[3,10,10,1]{3,2,1,0:T(8,128)S(1)}, u32[]{:S(2)}, u32[]{:S(2)}) %collective-permute-start.52) | collective-permute-done | bytes 1232 | tf_op jit(solution)/shard_map/ppermute | solution.py:29
  (161 shorter events, 174.6 us)
Async XLA Ops:
  1.7 12.7 %collective-permute-start = (f32[16,1,256]{2,1,0:T(1,128)S(1)}, f32[16,1,256]{2,1,0:T(1,128)S(1)}, u32[]{:S(2)}, u32[]{:S(2)}) collective-permute-start(f32[16,1,256]{2,1,0:T(1,128)S(1)} %get-tuple-element.26), channel_id=1, source_target_pairs={{0,256},{256,512},{512,768},{1,257},{257,513},{513,769},{2,258},{2... | collective-permute-start | bytes 49160 | tf_op jit(solution)/shard_map/ppermute | solution.py:28
  8.0 11.7 %collective-permute-start.3 = (f32[16,1,256]{2,1,0:T(1,128)S(1)}, f32[16,1,256]{2,1,0:T(1,128)S(1)}, u32[]{:S(2)}, u32[]{:S(2)}) collective-permute-start(f32[16,1,256]{2,1,0:T(1,128)S(1)} %get-tuple-element.28), channel_id=1, source_target_pairs={{0,256},{256,512},{512,768},{1,257},{257,513},{513,769},{2,258},{2... | collective-permute-start | bytes 49160 | tf_op jit(solution)/shard_map/ppermute | solution.py:28
  20.4 17.3 %collective-permute-start.5 = (f32[1,18,256]{2,1,0:T(8,128)S(1)}, f32[1,18,256]{2,1,0:T(8,128)S(1)}, u32[]{:S(2)}, u32[]{:S(2)}) collective-permute-start(f32[1,18,256]{2,1,0:T(8,128)S(1)} %get-tuple-element.23), channel_id=1, source_target_pairs={{32,0},{64,32},{96,64},{128,96},{160,128},{192,160},{224,192},{33,... | collective-permute-start | bytes 55304 | tf_op jit(solution)/shard_map/ppermute | solution.py:29
  23.5 14.2 %collective-permute-start.7 = (f32[1,18,256]{2,1,0:T(8,128)S(1)}, f32[1,18,256]{2,1,0:T(8,128)S(1)}, u32[]{:S(2)}, u32[]{:S(2)}) collective-permute-start(f32[1,18,256]{2,1,0:T(8,128)S(1)} %get-tuple-element.22), channel_id=1, source_target_pairs={{0,32},{32,64},{64,96},{96,128},{128,160},{160,192},{192,224},{1,3... | collective-permute-start | bytes 55304 | tf_op jit(solution)/shard_map/ppermute | solution.py:28
  25.9 24.5 %collective-permute-start.10 = (f32[18,18,1]{2,1,0:T(8,128)S(1)}, f32[18,18,1]{2,1,0:T(8,128)S(1)}, u32[]{:S(2)}, u32[]{:S(2)}) collective-permute-start(f32[18,18,1]{2,1,0:T(8,128)S(1)} %get-tuple-element.14), channel_id=1, source_target_pairs={{0,1},{1,2},{2,3},{3,4},{4,5},{5,6},{6,7},{7,8},{8,9},{9,10},{10,1... | collective-permute-start | bytes 3896 | tf_op jit(solution)/shard_map/ppermute | solution.py:28
  35.7 17.3 %collective-permute-start.8 = (f32[18,18,1]{2,1,0:T(8,128)S(1)}, f32[18,18,1]{2,1,0:T(8,128)S(1)}, u32[]{:S(2)}, u32[]{:S(2)}) collective-permute-start(f32[18,18,1]{2,1,0:T(8,128)S(1)} %get-tuple-element.15), channel_id=1, source_target_pairs={{1,0},{2,1},{3,2},{4,3},{5,4},{6,5},{7,6},{8,7},{9,8},{10,9},{11,1... | collective-permute-start | bytes 3896 | tf_op jit(solution)/shard_map/ppermute | solution.py:29
  38.8 19.1 %collective-permute-start.11 = (f32[18,18,1]{2,1,0:T(8,128)S(1)}, f32[18,18,1]{2,1,0:T(8,128)S(1)}, u32[]{:S(2)}, u32[]{:S(2)}) collective-permute-start(f32[18,18,1]{2,1,0:T(8,128)S(1)} %get-tuple-element.17), channel_id=1, source_target_pairs={{0,1},{1,2},{2,3},{3,4},{4,5},{5,6},{6,7},{7,8},{8,9},{9,10},{10,1... | collective-permute-start | bytes 3896 | tf_op jit(solution)/shard_map/ppermute | solution.py:28
  48.5 15.0 %collective-permute-start.9 = (f32[18,18,1]{2,1,0:T(8,128)S(1)}, f32[18,18,1]{2,1,0:T(8,128)S(1)}, u32[]{:S(2)}, u32[]{:S(2)}) collective-permute-start(f32[18,18,1]{2,1,0:T(8,128)S(1)} %get-tuple-element.16), channel_id=1, source_target_pairs={{1,0},{2,1},{3,2},{4,3},{5,4},{6,5},{7,6},{8,7},{9,8},{10,9},{11,1... | collective-permute-start | bytes 3896 | tf_op jit(solution)/shard_map/ppermute | solution.py:29
  80.6 19.5 %collective-permute-start.16 = (f32[18,18,1]{2,1,0:T(8,128)S(1)}, f32[18,18,1]{2,1,0:T(8,128)S(1)}, u32[]{:S(2)}, u32[]{:S(2)}) collective-permute-start(f32[18,18,1]{2,1,0:T(8,128)S(1)} %get-tuple-element.12), channel_id=1, source_target_pairs={{1,0},{2,1},{3,2},{4,3},{5,4},{6,5},{7,6},{8,7},{9,8},{10,9},{11,1... | collective-permute-start | bytes 3896 | tf_op jit(solution)/shard_map/ppermute | solution.py:29
  82.5 17.5 %collective-permute-start.17 = (f32[18,18,1]{2,1,0:T(8,128)S(1)}, f32[18,18,1]{2,1,0:T(8,128)S(1)}, u32[]{:S(2)}, u32[]{:S(2)}) collective-permute-start(f32[18,18,1]{2,1,0:T(8,128)S(1)} %get-tuple-element.13), channel_id=1, source_target_pairs={{0,1},{1,2},{2,3},{3,4},{4,5},{5,6},{6,7},{7,8},{8,9},{9,10},{10,1... | collective-permute-start | bytes 3896 | tf_op jit(solution)/shard_map/ppermute | solution.py:28
  127.6 31.0 %collective-permute-start.18 = (f32[8,1,128]{2,1,0:T(1,128)S(1)}, f32[8,1,128]{2,1,0:T(1,128)S(1)}, u32[]{:S(2)}, u32[]{:S(2)}) collective-permute-start(f32[8,1,128]{2,1,0:T(1,128)S(1)} %get-tuple-element.84), channel_id=1, source_target_pairs={{0,256},{256,512},{512,768},{1,257},{257,513},{513,769},{2,258},{2... | collective-permute-start | bytes 12296 | tf_op jit(solution)/shard_map/ppermute | solution.py:28
  129.6 29.1 %collective-permute-start.19 = (f32[8,1,128]{2,1,0:T(1,128)S(1)}, f32[8,1,128]{2,1,0:T(1,128)S(1)}, u32[]{:S(2)}, u32[]{:S(2)}) collective-permute-start(f32[8,1,128]{2,1,0:T(1,128)S(1)} %get-tuple-element.85), channel_id=1, source_target_pairs={{256,0},{512,256},{768,512},{257,1},{513,257},{769,513},{258,2},{5... | collective-permute-start | bytes 12296 | tf_op jit(solution)/shard_map/ppermute | solution.py:29
  165.8 11.9 %collective-permute-start.22 = (f32[10,10,1]{2,1,0:T(8,128)S(1)}, f32[10,10,1]{2,1,0:T(8,128)S(1)}, u32[]{:S(2)}, u32[]{:S(2)}) collective-permute-start(f32[10,10,1]{2,1,0:T(8,128)S(1)} %get-tuple-element.75), channel_id=1, source_target_pairs={{0,1},{1,2},{2,3},{3,4},{4,5},{5,6},{6,7},{7,8},{8,9},{9,10},{10,1... | collective-permute-start | bytes 1208 | tf_op jit(solution)/shard_map/ppermute | solution.py:28
  174.6 12.6 %collective-permute-start.23 = (f32[10,10,1]{2,1,0:T(8,128)S(1)}, f32[10,10,1]{2,1,0:T(8,128)S(1)}, u32[]{:S(2)}, u32[]{:S(2)}) collective-permute-start(f32[10,10,1]{2,1,0:T(8,128)S(1)} %get-tuple-element.76), channel_id=1, source_target_pairs={{1,0},{2,1},{3,2},{4,3},{5,4},{6,5},{7,6},{8,7},{9,8},{10,9},{11,1... | collective-permute-start | bytes 1208 | tf_op jit(solution)/shard_map/ppermute | solution.py:29
  204.3 14.5 %collective-permute-start.29 = (f32[3,10,10,1]{3,2,1,0:T(8,128)S(1)}, f32[3,10,10,1]{3,2,1,0:T(8,128)S(1)}, u32[]{:S(2)}, u32[]{:S(2)}) collective-permute-start(f32[3,10,10,1]{3,2,1,0:T(8,128)S(1)} %get-tuple-element.39), channel_id=1, source_target_pairs={{0,1},{1,2},{2,3},{3,4},{4,5},{5,6},{6,7},{7,8},{8,9},{9,10},{10,1... | collective-permute-start | bytes 3608 | tf_op jit(solution)/shard_map/ppermute | solution.py:28
  208.4 16.2 %collective-permute-start.28 = (f32[3,10,10,1]{3,2,1,0:T(8,128)S(1)}, f32[3,10,10,1]{3,2,1,0:T(8,128)S(1)}, u32[]{:S(2)}, u32[]{:S(2)}) collective-permute-start(f32[3,10,10,1]{3,2,1,0:T(8,128)S(1)} %get-tuple-element.38), channel_id=1, source_target_pairs={{1,0},{2,1},{3,2},{4,3},{5,4},{6,5},{7,6},{8,7},{9,8},{10,9},{11,1... | collective-permute-start | bytes 3608 | tf_op jit(solution)/shard_map/ppermute | solution.py:29
  242.7 15.7 %collective-permute-start.35 = (f32[3,10,10,1]{3,2,1,0:T(8,128)S(1)}, f32[3,10,10,1]{3,2,1,0:T(8,128)S(1)}, u32[]{:S(2)}, u32[]{:S(2)}) collective-permute-start(f32[3,10,10,1]{3,2,1,0:T(8,128)S(1)} %get-tuple-element.37), channel_id=1, source_target_pairs={{0,1},{1,2},{2,3},{3,4},{4,5},{5,6},{6,7},{7,8},{8,9},{9,10},{10,1... | collective-permute-start | bytes 3608 | tf_op jit(solution)/shard_map/ppermute | solution.py:28
  250.4 16.3 %collective-permute-start.34 = (f32[3,10,10,1]{3,2,1,0:T(8,128)S(1)}, f32[3,10,10,1]{3,2,1,0:T(8,128)S(1)}, u32[]{:S(2)}, u32[]{:S(2)}) collective-permute-start(f32[3,10,10,1]{3,2,1,0:T(8,128)S(1)} %get-tuple-element.36), channel_id=1, source_target_pairs={{1,0},{2,1},{3,2},{4,3},{5,4},{6,5},{7,6},{8,7},{9,8},{10,9},{11,1... | collective-permute-start | bytes 3608 | tf_op jit(solution)/shard_map/ppermute | solution.py:29
  282.0 14.2 %collective-permute-start.41 = (f32[3,10,10,1]{3,2,1,0:T(8,128)S(1)}, f32[3,10,10,1]{3,2,1,0:T(8,128)S(1)}, u32[]{:S(2)}, u32[]{:S(2)}) collective-permute-start(f32[3,10,10,1]{3,2,1,0:T(8,128)S(1)} %get-tuple-element.35), channel_id=1, source_target_pairs={{0,1},{1,2},{2,3},{3,4},{4,5},{5,6},{6,7},{7,8},{8,9},{9,10},{10,1... | collective-permute-start | bytes 3608 | tf_op jit(solution)/shard_map/ppermute | solution.py:28
  289.1 15.8 %collective-permute-start.40 = (f32[3,10,10,1]{3,2,1,0:T(8,128)S(1)}, f32[3,10,10,1]{3,2,1,0:T(8,128)S(1)}, u32[]{:S(2)}, u32[]{:S(2)}) collective-permute-start(f32[3,10,10,1]{3,2,1,0:T(8,128)S(1)} %get-tuple-element.34), channel_id=1, source_target_pairs={{1,0},{2,1},{3,2},{4,3},{5,4},{6,5},{7,6},{8,7},{9,8},{10,9},{11,1... | collective-permute-start | bytes 3608 | tf_op jit(solution)/shard_map/ppermute | solution.py:29
  319.2 12.9 %collective-permute-start.47 = (f32[3,10,10,1]{3,2,1,0:T(8,128)S(1)}, f32[3,10,10,1]{3,2,1,0:T(8,128)S(1)}, u32[]{:S(2)}, u32[]{:S(2)}) collective-permute-start(f32[3,10,10,1]{3,2,1,0:T(8,128)S(1)} %get-tuple-element.33), channel_id=1, source_target_pairs={{0,1},{1,2},{2,3},{3,4},{4,5},{5,6},{6,7},{7,8},{8,9},{9,10},{10,1... | collective-permute-start | bytes 3608 | tf_op jit(solution)/shard_map/ppermute | solution.py:28
  325.8 13.5 %collective-permute-start.46 = (f32[3,10,10,1]{3,2,1,0:T(8,128)S(1)}, f32[3,10,10,1]{3,2,1,0:T(8,128)S(1)}, u32[]{:S(2)}, u32[]{:S(2)}) collective-permute-start(f32[3,10,10,1]{3,2,1,0:T(8,128)S(1)} %get-tuple-element.32), channel_id=1, source_target_pairs={{1,0},{2,1},{3,2},{4,3},{5,4},{6,5},{7,6},{8,7},{9,8},{10,9},{11,1... | collective-permute-start | bytes 3608 | tf_op jit(solution)/shard_map/ppermute | solution.py:29
  355.0 12.8 %collective-permute-start.53 = (f32[3,10,10,1]{3,2,1,0:T(8,128)S(1)}, f32[3,10,10,1]{3,2,1,0:T(8,128)S(1)}, u32[]{:S(2)}, u32[]{:S(2)}) collective-permute-start(f32[3,10,10,1]{3,2,1,0:T(8,128)S(1)} %get-tuple-element.31), channel_id=1, source_target_pairs={{0,1},{1,2},{2,3},{3,4},{4,5},{5,6},{6,7},{7,8},{8,9},{9,10},{10,1... | collective-permute-start | bytes 3608 | tf_op jit(solution)/shard_map/ppermute | solution.py:28
  362.2 16.2 %collective-permute-start.52 = (f32[3,10,10,1]{3,2,1,0:T(8,128)S(1)}, f32[3,10,10,1]{3,2,1,0:T(8,128)S(1)}, u32[]{:S(2)}, u32[]{:S(2)}) collective-permute-start(f32[3,10,10,1]{3,2,1,0:T(8,128)S(1)} %get-tuple-element.30), channel_id=1, source_target_pairs={{1,0},{2,1},{3,2},{4,3},{5,4},{6,5},{7,6},{8,7},{9,8},{10,9},{11,1... | collective-permute-start | bytes 3608 | tf_op jit(solution)/shard_map/ppermute | solution.py:29
  (31 other events, 208.0 us)
where the time goes:
time: 382 us; the launch traced here: 379 us
  starting transfers between devices  189 us (49%)
  waiting for transfers between devices  123 us (32%)
  local copies, waits for them, and re-layouts  39.1 us (10%)
  other arithmetic  26.4 us (7%)
    ppermute x27, starting transfers between devices, padded_2(): before = lax.ppermute(last, axis, up)  108 us
    ppermute x27, starting transfers between devices, padded_2(): after = lax.ppermute(initial, axis, down)  80.9 us
    ppermute x27, waiting for transfers between devices, padded_2(): after = lax.ppermute(initial, axis, down)  71.2 us
    ppermute x27, waiting for transfers between devices, padded_2(): before = lax.ppermute(last, axis, up)  51.4 us
    reshape x2, local copies, waits for them, and re-layouts, merge_blocks(): field.reshape(vertical_span // 2, 2, count_across_north // 2, 2, count_ac...  36.2 us
    reduce_sum x2, other arithmetic, merge_blocks(): return jnp.sum(blocks, axis=(1, 3, 5)) * 0.125  14 us
  transfers between devices with their start and end apart: 54, of which 29 were waited for; matrix products, arithmetic and copies ran while one was open for 8% of the time, Pallas kernels for 0%

commit v1 on v0

v1 whole, which is shorter than its diff:
```python
import functools

import jax
import jax.numpy as jnp
from jax import lax
from jax.experimental import pallas as pl
from jax.experimental.pallas import tpu as pltpu
from jax.sharding import PartitionSpec as P

SWEEPS = 6
time_step = 0.15
spot_power = 30.0
shear_modulus = 1.0
coupling = 1.5
stress_factor = 8.0
eigen_low = 0.5
eigen_high = 3.5

MESH = pl.DeviceIdType.MESH
OUTSIDE = -4.0

DIRS = [(1, 0), (-1, 0), (0, 1), (0, -1), (1, 1), (1, -1), (-1, 1), (-1, -1)]

f32 = jnp.float32
bf16 = jnp.bfloat16


def lanes(n):
    return lax.broadcasted_iota(jnp.int32, (8, n), 1)


def conductance(s):
    return jnp.maximum(jnp.maximum(s * (2.0 / 15.0) + 0.2, s * (2.0 / 3.0) - (1.0 / 3.0)), 0.0)


def conductances(e_ref, g_ref):
    planes, rows, width = e_ref.shape[1:]

    def body(z, _):
        f = e_ref[0, z]
        up = e_ref[0, jnp.minimum(z + 1, planes - 1)]
        g_ref[0, z] = conductance(f + pltpu.roll(f, width - 1, 1))
        g_ref[1, z] = conductance(f + pltpu.roll(f, rows - 1, 0))
        g_ref[2, z] = conductance(f + up)
        g_ref[3, z] = (2.0 * time_step) - time_step * f
        return 0

    lax.fori_loop(0, planes, body, 0)


def thermal(t_in, t_out, g_ref, source, first, last):
    rows, width = g_ref.shape[2:]

    def body(z, _):
        t = t_in[z]
        fx = g_ref[0, z] * (pltpu.roll(t, width - 1, 1) - t)
        fy = g_ref[1, z] * (pltpu.roll(t, rows - 1, 0) - t)
        fz = g_ref[2, z] * (t_in[z + 1] - t)
        fb = g_ref[2, z - 1] * (t - t_in[z - 1])
        total = (fx - pltpu.roll(fx, 1, 1)) + (fy - pltpu.roll(fy, 1, 0)) + (fz - fb)
        t_out[z] = t + g_ref[3, z] * total
        return 0

    lax.fori_loop(first, last, body, 0)
    t_out[17] = t_out[17] + g_ref[3, 17] * source


def laser(by_ref, bx_ref, substep, ypos, xpos, scale):
    total = jnp.zeros(ypos.shape, f32)
    for p in range(4):
        hit = (ypos == by_ref[substep, p]) & (xpos == bx_ref[substep, p])
        total = total + jnp.where(hit, scale, 0.0)
    return total


def kernel(w_hbm, f_hbm, by_ref, bx_ref, t_out, u_out,
           w_v, f_v, em, ew, gm, gw, t1m, t1w, t2m, t2w,
           zs, zr, ys, yr, ds, dr, xs, xr, qs, cb, czr, cyr, cdr,
           cx, dira, dirb, res, inv, spr, div, pick, t_v,
           load_sem, send_sem, recv_sem, out_sem):
    me = {a: lax.axis_index(a) for a in ("slab", "grp", "brick")}
    size = {a: lax.axis_size(a) for a in ("slab", "grp", "brick")}

    def has(off):
        found = None
        for a, d in zip(("slab", "grp", "brick"), off):
            if d:
                one = me[a] < size[a] - 1 if d > 0 else me[a] > 0
                found = one if found is None else found & one
        return found

    def device(off):
        return {a: me[a] + d for a, d in zip(("slab", "grp", "brick"), off)}

    def negative(off):
        return tuple(-d for d in off)

    neighbours = [d + (0,) for d in DIRS] + [(0, 0, 1), (0, 0, -1)]

    barrier = pltpu.get_barrier_semaphore()
    count = jnp.int32(0)
    for off in neighbours:
        @pl.when(has(off))
        def _(off=off):
            pl.semaphore_signal(barrier, inc=1, device_id=device(off), device_id_type=MESH)
        count = count + has(off).astype(jnp.int32)

    load_w = pltpu.make_async_copy(w_hbm, w_v, load_sem.at[0])
    load_f = pltpu.make_async_copy(f_hbm, f_v, load_sem.at[1])
    load_w.start()
    load_f.start()

    k = lax.broadcasted_iota(jnp.int32, (384, 256), 0)
    c = lax.broadcasted_iota(jnp.int32, (384, 256), 1)
    h = c - 128
    base = jnp.where(c < 128, 2 * c, jnp.where(h < 64, 256 + 32 + 2 * h, 256 + 2 * h - 160))
    used = (c < 128) | (h < 8) | (h >= 120)
    pick[...] = jnp.where(used & ((k == base) | (k == base + 1)), 1.0, 0.0).astype(bf16)

    on_top = jnp.where(me["slab"] == size["slab"] - 1, spot_power, 0.0).astype(f32)
    y0 = me["grp"] * 16 - 4
    x0 = me["brick"] * 256
    ym = lax.broadcasted_iota(jnp.int32, (24, 256), 0) + y0
    xm = lax.broadcasted_iota(jnp.int32, (24, 256), 1) + x0
    yw = lax.broadcasted_iota(jnp.int32, (24, 128), 0) + y0
    lw = lax.broadcasted_iota(jnp.int32, (24, 128), 1)
    xw = jnp.where(lw < 64, lw + 224, lw - 96) + x0

    em[:, 0:2] = jnp.zeros((2, 2, 24, 256), f32)
    em[:, 18:20] = jnp.zeros((2, 2, 24, 256), f32)

    load_f.wait()
    load_w.wait()
    edge = jnp.zeros((16, 4, 256), f32)
    em[0, 2:18] = jnp.concatenate([edge, f_v[...].astype(f32), edge], axis=1)
    em[1, 2:18] = jnp.concatenate([edge, w_v[...], edge], axis=1)
    for i, z in ((0, 14), (1, 0)):
        zs[i, 0] = f_v[z : z + 2].astype(f32)
        zs[i, 1] = w_v[z : z + 2]
        ys[i, 0] = f_v[:, z : z + 2, :].astype(f32)
        ys[i, 1] = w_v[:, z : z + 2, :]
    for i, (dz, dy) in enumerate(DIRS[4:]):
        z, y = (15 if dz > 0 else 0), (15 if dy > 0 else 0)
        ds[i, 0:1] = f_v[z, y : y + 1, :].astype(f32)
        ds[i, 1:2] = w_v[z, y : y + 1, :]

    pl.semaphore_wait(barrier, count)

    def copy(source, target, slot, off):
        return pltpu.make_async_remote_copy(
            src_ref=source, dst_ref=target, send_sem=send_sem.at[slot], recv_sem=recv_sem.at[slot],
            device_id=device(off), device_id_type=MESH)

    def start(messages):
        for source, target, slot, off, fill in messages:
            @pl.when(has(off))
            def _(source=source, target=target, slot=slot, off=off):
                copy(source, target, slot, off).start()

    def receive(messages):
        for source, target, slot, off, fill in messages:
            there = has(negative(off))

            @pl.when(there)
            def _(source=source, target=target, slot=slot, off=off):
                copy(source, target, slot, off).wait_recv()

            @pl.when(jnp.logical_not(there))
            def _(target=target, fill=fill):
                fill(target)

    def sent(messages):
        for source, target, slot, off, fill in messages:
            @pl.when(has(off))
            def _(source=source, target=target, slot=slot, off=off):
                copy(source, target, slot, off).wait_send()

    def fill_pair(target):
        shape = target.shape[1:]
        target[0] = jnp.full(shape, OUTSIDE, f32)
        target[1] = jnp.zeros(shape, f32)

    def fill_row(target):
        row = lax.broadcasted_iota(jnp.int32, (2, 256), 0)
        target[...] = jnp.where(row == 0, OUTSIDE, 0.0).astype(f32)

    raw = []
    for slot, d in enumerate(DIRS):
        off = d + (0,)
        if slot < 2:
            raw.append((zs.at[slot], zr.at[slot], slot, off, fill_pair))
        elif slot < 4:
            raw.append((ys.at[slot - 2], yr.at[slot - 2], slot, off, fill_pair))
        else:
            raw.append((ds.at[slot - 4], dr.at[slot - 4], slot, off, fill_row))
    start(raw)
    receive(raw)

    em[:, 0:2, 4:20, :] = zr[0]
    em[:, 18:20, 4:20, :] = zr[1]
    em[:, 2:18, 2:4, :] = yr[0]
    em[:, 2:18, 20:22, :] = yr[1]
    for i, (dz, dy) in enumerate(DIRS[4:]):
        z, y = (1 if dz > 0 else 18), (3 if dy > 0 else 20)
        for f in range(2):
            em[f, z, y : y + 1, :] = dr[i, f : f + 1, :]

    slot_of = lanes(128) // 16
    for f in range(2):
        for v in range(8):
            right, left = jnp.zeros((8, 128), f32), jnp.zeros((8, 128), f32)
            for j in range(8):
                r = 8 * v + j
                if r < 60:
                    z, y = r // 3, 8 * (r % 3)
                    right = jnp.where(slot_of == j, pltpu.roll(em[f, z, y : y + 8, 128:256], (16 * j - 112) % 128, 1), right)
                    left = jnp.where(slot_of == j, pltpu.roll(em[f, z, y : y + 8, 0:128], 16 * j, 1) if j else em[f, z, y : y + 8, 0:128], left)
            xs[0, f, v] = right
            xs[1, f, v] = left
    along = [(xs.at[i], xr.at[i], 8 + i, (0, 0, 1 - 2 * i), fill_pair) for i in range(2)]
    start(along)

    conductances(em, gm)
    thermal(em.at[1], t1m, gm, laser(by_ref, bx_ref, 0, ym, xm, on_top), 1, 19)
    thermal(t1m, t2m, gm, laser(by_ref, bx_ref, 1, ym, xm, on_top), 2, 18)

    receive(along)
    lane = lanes(128)
    for f in range(2):
        for r in range(60):
            v, j = r // 8, r % 8
            z, y = r // 3, 8 * (r % 3)
            own = jnp.where(lane < 64, pltpu.roll(em[f, z, y : y + 8, 128:256], 32, 1), pltpu.roll(em[f, z, y : y + 8, 0:128], 96, 1))
            before, after = xr[0, f, v], xr[1, f, v]
            before = pltpu.roll(before, (80 - 16 * j) % 128, 1) if (80 - 16 * j) % 128 else before
            after = pltpu.roll(after, (32 - 16 * j) % 128, 1) if (32 - 16 * j) % 128 else after
            own = jnp.where((lane >= 32) & (lane < 48), after, own)
            ew[f, z, y : y + 8, :] = jnp.where((lane >= 80) & (lane < 96), before, own)
    conductances(ew, gw)
    thermal(ew.at[1], t1w, gw, laser(by_ref, bx_ref, 0, yw, xw, on_top), 1, 19)
    thermal(t1w, t2w, gw, laser(by_ref, bx_ref, 1, yw, xw, on_top), 2, 18)

    lane16 = lax.broadcasted_iota(jnp.int32, (16, 128), 1)

    def merge(zp, _):
        sums = [None] * 6
        for d in range(2):
            z = 2 * zp + d
            w = t2w[z + 2, 4:20, :]
            a = jnp.where(lane16 < 16, pltpu.roll(w, 32, 1), t2m[z + 2, 4:20, 0:128])
            b = jnp.where(lane16 >= 112, pltpu.roll(w, 96, 1), t2m[z + 2, 4:20, 128:256])
            t_v[z, :, 0:128] = a
            t_v[z, :, 128:256] = b
            fa, fb, fw = em[0, z + 2, 4:20, 0:128], em[0, z + 2, 4:20, 128:256], ew[0, z + 2, 4:20, :]
            for i, piece in enumerate((fa * a, fb * b, fw * w, fa, fb, fw)):
                sums[i] = piece if sums[i] is None else sums[i] + piece
        for i in range(6):
            qs[i // 3, i % 3, zp] = sums[i]
        return 0

    lax.fori_loop(0, 8, merge, 0)
    save = pltpu.make_async_copy(t_v, t_out, out_sem.at[0])
    save.start()

    rows = []
    for f in range(2):
        tiles = [
            (qs[f, t, :, pl.ds(0, 8, stride=2), :] + qs[f, t, :, pl.ds(1, 8, stride=2), :]).reshape(64, 128)
            for t in range(3)
        ]
        rows.append(jnp.concatenate(tiles, axis=1) * 0.125)
    q, solid = rows
    q1 = q.astype(bf16)
    rest = q - q1.astype(f32)
    q2 = rest.astype(bf16)
    q3 = (rest - q2.astype(f32)).astype(bf16)
    coarse = jnp.dot(jnp.concatenate([q1, q2, q3, solid.astype(bf16)], axis=0), pick[...], preferred_element_type=f32)
    strain = (coarse[0:64] + coarse[64:128]) + coarse[128:192]
    fields = [strain.reshape(8, 8, 256), coarse[192:256].reshape(8, 8, 256)]
    for f in range(2):
        packed = jnp.zeros((8, 128), f32)
        for z in range(8):
            packed = jnp.where(slot_of == z, pltpu.roll(fields[f][z, :, 128:256], (8 + 16 * z) % 128, 1), packed)
            cb[f, 1 + z] = fields[f][z, :, 0:128]
            cx[f, 6 + z, 8:16, :] = fields[f][z]
        cb[f, 0] = packed
        cb[f, 9] = packed

    def fill_coarse(target):
        shape = target.shape[1:]
        target[0] = jnp.zeros(shape, f32)
        target[1] = jnp.full(shape, OUTSIDE, f32)

    last6, first6 = cb.at[:, 3:10], cb.at[:, 0:7]
    swap = []
    for slot, d in enumerate(DIRS):
        off = d + (0,)
        if slot < 2:
            source, target = (last6, first6)[slot], czr.at[slot]
        elif slot < 4:
            source, target = cb.at[:, 0:9], cyr.at[slot - 2]
        else:
            source, target = (last6 if d[0] > 0 else first6), cdr.at[slot - 4]
        swap.append((source, target, 10 + slot, off, fill_coarse))
    start(swap)
    receive(swap)

    rim = (lane < 8) | (lane >= 120)

    def place(block, f, first_plane, zs_, packed, tile):
        p = block[f, packed]
        for i, z in enumerate(zs_):
            at = first_plane[1] + i
            cx[f, at, 8 * tile : 8 * tile + 8, 0:128] = block[f, first_plane[0] + i]
            back = (-(8 + 16 * z)) % 128
            cx[f, at, 8 * tile : 8 * tile + 8, 128:256] = jnp.where(rim, pltpu.roll(p, back, 1) if back else p, 0.0)

    upper, lower = range(2, 8), range(0, 6)
    for f in range(2):
        place(czr.at[0], f, (0, 0), upper, 6, 1)
        place(czr.at[1], f, (1, 14), lower, 0, 1)
        place(cyr.at[0], f, (1, 6), range(8), 0, 0)
        place(cyr.at[1], f, (1, 6), range(8), 0, 2)
        for i, (dz, dy) in enumerate(DIRS[4:]):
            if dz > 0:
                place(cdr.at[i], f, (0, 0), upper, 6, 0 if dy > 0 else 2)
            else:
                place(cdr.at[i], f, (1, 14), lower, 0, 0 if dy > 0 else 2)

    sweeps(cx, u_out, dira, dirb, res, inv, spr, div)
    save.wait()
    sent(raw)
    sent(along)
    sent(swap)


def sweeps(cx, u_out, dira, dirb, res, inv, spr, div):
    centre_value = (eigen_high + eigen_low) / 2.0
    radius = (eigen_high - eigen_low) / 2.0
    sigma = centre_value / radius
    rho = 1.0 / sigma
    half = 0.5 * stress_factor
    next_x = lambda a: pltpu.roll(a, 255, 1)
    prev_x = lambda a: pltpu.roll(a, 1, 1)
    next_y = lambda a: pltpu.roll(a, 23, 0)
    prev_y = lambda a: pltpu.roll(a, 1, 0)

    def begin(z, _):
        solid = cx[1, z]
        spring = 0.5 + 1.5 * solid
        inverse = jnp.where(solid < -1.0, 0.0, 1.0 / (6.0 * shear_modulus + 2.0 * coupling + spring))
        inv[z] = inverse
        spr[z] = spring + 6.0 * shear_modulus
        s = cx[0, z]
        force = (half * (cx[0, z - 1] - cx[0, z + 1]), half * (prev_y(s) - next_y(s)), half * (prev_x(s) - next_x(s)))
        for d in range(3):
            res[d, z] = force[d]
            dira[d, z] = force[d] * inverse * (1.0 / centre_value)
        return 0

    lax.fori_loop(1, 19, begin, 0)
    for d in range(3):
        u_out[d] = dira[d, 6:14, 8:16, 0:128]

    old, new = dira, dirb
    for sweep in range(SWEEPS - 1):
        halo = SWEEPS - 2 - sweep
        rho_next = 1.0 / (2.0 * sigma - rho)
        keep, gain = rho_next * rho, 2.0 * rho_next / radius

        def spread(z, _, old=old):
            a, b, c = old[0, z], old[1, z], old[2, z]
            div[z] = (old[0, z + 1] - a) + (next_y(b) - b) + (next_x(c) - c)
            return 0

        lax.fori_loop(6 - halo - 1, 14 + halo, spread, 0)

        def step(z, _, old=old, new=new, keep=keep, gain=gain):
            here = div[z]
            back = (div[z - 1] - here, prev_y(here) - here, prev_x(here) - here)
            factor, inverse = spr[z], inv[z] * gain
            for d in range(3):
                v = old[d, z]
                around = (old[d, z + 1] + old[d, z - 1]) + (next_y(v) + prev_y(v)) + (next_x(v) + prev_x(v))
                r = res[d, z] - (factor * v - shear_modulus * around + coupling * back[d])
                res[d, z] = r
                new[d, z] = keep * v + inverse * r
            return 0

        lax.fori_loop(6 - halo, 14 + halo, step, 0)
        for d in range(3):
            u_out[d] = u_out[d] + new[d, 6:14, 8:16, 0:128]
        rho = rho_next
        old, new = new, old


def per_device(warmth, flag, north, east):
    vmem = pltpu.VMEM
    ext = lambda *s: vmem(s, f32)
    scratch = [
        ext(16, 16, 256), vmem((16, 16, 256), jnp.int32),
        ext(2, 20, 24, 256), ext(2, 20, 24, 128), ext(4, 20, 24, 256), ext(4, 20, 24, 128),
        ext(20, 24, 256), ext(20, 24, 128), ext(20, 24, 256), ext(20, 24, 128),
        ext(2, 2, 2, 16, 256), ext(2, 2, 2, 16, 256), ext(2, 2, 16, 2, 256), ext(2, 2, 16, 2, 256), ext(4, 2, 256), ext(4, 2, 256),
        ext(2, 2, 8, 8, 128), ext(2, 2, 8, 8, 128), ext(2, 3, 8, 16, 128),
        ext(2, 10, 8, 128), ext(2, 2, 7, 8, 128), ext(2, 2, 9, 8, 128), ext(4, 2, 7, 8, 128),
        ext(2, 20, 24, 256), ext(3, 20, 24, 256), ext(3, 20, 24, 256), ext(3, 20, 24, 256), ext(20, 24, 256), ext(20, 24, 256), ext(20, 24, 256),
        vmem((384, 256), bf16), ext(16, 16, 256),
        pltpu.SemaphoreType.DMA((2,)), pltpu.SemaphoreType.DMA((18,)), pltpu.SemaphoreType.DMA((18,)), pltpu.SemaphoreType.DMA((1,)),
    ]
    return pl.pallas_call(
        kernel,
        out_shape=(jax.ShapeDtypeStruct((16, 16, 256), f32), jax.ShapeDtypeStruct((3, 8, 8, 128), f32)),
        in_specs=[
            pl.BlockSpec(memory_space=pl.ANY),
            pl.BlockSpec(memory_space=pl.ANY),
            pl.BlockSpec(memory_space=pltpu.SMEM),
            pl.BlockSpec(memory_space=pltpu.SMEM),
        ],
        out_specs=(pl.BlockSpec(memory_space=pl.ANY), pl.BlockSpec(memory_space=pltpu.VMEM)),
        scratch_shapes=scratch,
        compiler_params=pltpu.CompilerParams(collective_id=0, has_side_effects=True),
    )(warmth, flag, north, east)


def solution(mesh):
    in_specs = (P("slab", "grp", "brick"), P("slab", "grp", "brick"), P(), P())
    out_specs = (P("slab", "grp", "brick"), P(None, "slab", "grp", "brick"))
    return jax.shard_map(per_device, mesh=mesh, in_specs=in_specs, out_specs=out_specs, check_vma=False)
```

time: 382 us -> 57.6 us (0.15)
  the two profiles are of different devices: /device:TPU:493 before, /device:TPU:2 now
where the time goes in v1:
time: 57.6 us; the launch traced here: 57.4 us
  Pallas kernels  54.4 us (94%)
  local copies, waits for them, and re-layouts  2.35 us (4%)
  between operations  0.65 us (1%)
    pallas_call x1, Pallas kernels, per_device(): pl.pallas_call(kernel, out_shape=(jax.ShapeDtypeStruct((16, 16, 256), f32...  54.4 us
    unnamed x4, local copies, waits for them, and re-layouts  2.35 us

profile of v1, /device:TPU:2, one launch (start us, length us, event | category | flops | bytes accessed | tf_op | source)
XLA Modules:
  0.0 57.4 jit_solution(17705815024753983907)
XLA Ops:
  0.6 54.4 %shard_map.59 = (f32[16,16,256]{2,1,0:T(8,128)}, f32[3,8,8,128]{3,2,1,0:T(8,128)}) custom-call(f32[16,16,256]{2,1,0:T(8,128)} %w_hbm.1, s32[16,16,256]{2,1,0:T(8,128)} %f_hbm.1, s32[2,4]{1,0:T(2,128)} %by_ref.1, s32[2,4]{1,0:T(2,128)} %bx_ref.1), custom_call_target="tpu_custom_call" | custom-call | tf_op jit(solution)/shard_map/pallas_call | solution.py:411
  55.0 0.0 copy-start
  55.0 1.7 %copy.8 = f32[16,16,256]{2,1,0:T(8,128)} copy(f32[16,16,256]{2,1,0:T(8,128)} %get-tuple-element.4) | data formatting | bytes 524288
  56.7 0.0 copy-done
  56.7 0.6 %copy.9 = f32[3,8,8,128]{3,2,1,0:T(8,128)} copy(f32[3,8,8,128]{3,2,1,0:T(8,128)S(1)} %copy-done) | data formatting | bytes 196608
Async XLA Ops:
  55.0 1.7 %copy-start = (f32[3,8,8,128]{3,2,1,0:T(8,128)S(1)}, f32[3,8,8,128]{3,2,1,0:T(8,128)}, u32[]{:S(2)}) copy-start(f32[3,8,8,128]{3,2,1,0:T(8,128)} %get-tuple-element.5) | copy-start | bytes 294916

commit v2 on v1

v2 whole, which is shorter than its diff:
```python
import functools

import jax
import jax.numpy as jnp
from jax import lax
from jax.experimental import pallas as pl
from jax.experimental.pallas import tpu as pltpu
from jax.sharding import PartitionSpec as P

SWEEPS = 6
time_step = 0.15
spot_power = 30.0
shear_modulus = 1.0
coupling = 1.5
stress_factor = 8.0
eigen_low = 0.5
eigen_high = 3.5

MESH = pl.DeviceIdType.MESH
OUTSIDE = -4.0

DIRS = [(1, 0), (-1, 0), (0, 1), (0, -1), (1, 1), (1, -1), (-1, 1), (-1, -1)]

f32 = jnp.float32
bf16 = jnp.bfloat16


def lane_of(rows):
    return lax.broadcasted_iota(jnp.int32, (rows, 128), 1)


def next_x(tiles):
    rolled = [pltpu.roll(t, 127, 1) for t in tiles]
    if len(tiles) == 1:
        return rolled
    end = lane_of(tiles[0].shape[0]) == 127
    return [jnp.where(end, rolled[1 - i], rolled[i]) for i in range(2)]


def prev_x(tiles):
    rolled = [pltpu.roll(t, 1, 1) for t in tiles]
    if len(tiles) == 1:
        return rolled
    end = lane_of(tiles[0].shape[0]) == 0
    return [jnp.where(end, rolled[1 - i], rolled[i]) for i in range(2)]


def conductance(s):
    return jnp.maximum(jnp.maximum(s * (2.0 / 15.0) + 0.2, s * (2.0 / 3.0) - (1.0 / 3.0)), 0.0)


def conductances(e, g, tiles):
    for z in range(19):
        f = [e[0, t, z, 2:26, :] for t in tiles]
        fx = next_x(f) if z else None
        for i, t in enumerate(tiles):
            g[2, t, z, 2:26, :] = conductance(f[i] + e[0, t, z + 1, 2:26, :])
            if z:
                g[0, t, z, 2:26, :] = conductance(f[i] + fx[i])
                g[1, t, z, 2:26, :] = conductance(f[i] + e[0, t, z, 3:27, :])
                g[3, t, z, 2:26, :] = (2.0 * time_step) - time_step * f[i]


def thermal(t_in, t_out, g, source, tiles, first, last, r, n):
    below = [g[2, t, first - 1, r : r + n, :] * (t_in(t, first, r) - t_in(t, first - 1, r)) for t in tiles]
    for z in range(first, last):
        here = [t_in(t, z, r) for t in tiles]
        ahead = next_x(here)
        fx = [g[0, t, z, r : r + n, :] * (ahead[i] - here[i]) for i, t in enumerate(tiles)]
        back = prev_x(fx)
        for i, t in enumerate(tiles):
            fy = g[1, t, z, r : r + n, :] * (t_in(t, z, r + 1) - here[i])
            by = g[1, t, z, r - 1 : r + n - 1, :] * (here[i] - t_in(t, z, r - 1))
            fz = g[2, t, z, r : r + n, :] * (t_in(t, z + 1, r) - here[i])
            total = (fx[i] - back[i]) + (fy - by) + (fz - below[i])
            if z == 17:
                total = total + source[i]
            t_out(t, z, here[i] + g[3, t, z, r : r + n, :] * total)
            below[i] = fz


def kernel(w_hbm, f_hbm, by_hbm, bx_hbm, t_out, u_out,
           w_v, f_v, by_ref, bx_ref, e, g, t1, t2,
           zs, zr, ys, yr, ds, dr, xs, xr, qs, cbm, cbw, czr, cyr, cdr, cwr,
           cx, dira, dirb, res, inv, spr, div, pick_m, pick_w, t_v, u_v,
           load_sem, send_sem, recv_sem, out_sem):
    me = {a: lax.axis_index(a) for a in ("slab", "grp", "brick")}
    size = {a: lax.axis_size(a) for a in ("slab", "grp", "brick")}

    def has(off):
        found = None
        for a, d in zip(("slab", "grp", "brick"), off):
            if d:
                one = me[a] < size[a] - 1 if d > 0 else me[a] > 0
                found = one if found is None else found & one
        return found

    def device(off):
        return {a: me[a] + d for a, d in zip(("slab", "grp", "brick"), off)}

    def negative(off):
        return tuple(-d for d in off)

    loads = [
        pltpu.make_async_copy(source, target, load_sem.at[i])
        for i, (source, target) in enumerate(((f_hbm, f_v), (w_hbm, w_v), (by_hbm, by_ref), (bx_hbm, bx_ref)))
    ]
    for load in loads:
        load.start()

    neighbours = [d + (0,) for d in DIRS] + [(0, 0, 1), (0, 0, -1)]
    barrier = pltpu.get_barrier_semaphore()
    count = jnp.int32(0)
    for off in neighbours:
        @pl.when(has(off))
        def _(off=off):
            pl.semaphore_signal(barrier, inc=1, device_id=device(off), device_id_type=MESH)
        count = count + has(off).astype(jnp.int32)

    k = lax.broadcasted_iota(jnp.int32, (256, 128), 0)
    c = lax.broadcasted_iota(jnp.int32, (256, 128), 1)
    pick_m[...] = jnp.where(k // 2 == c, 1.0, 0.0).astype(bf16)
    k, j = k[0:128], c[0:128] % 16
    start_w = jnp.where(j < 7, 84 + 2 * j, 16 + 2 * j)
    pick_w[...] = jnp.where((j < 14) & ((k == start_w) | (k == start_w + 1)), 1.0, 0.0).astype(bf16)

    for t in range(2):
        for f in range(2):
            e[f, t, 0:2] = jnp.zeros((2, 32, 128), f32)
            e[f, t, 18:20] = jnp.zeros((2, 32, 128), f32)
            e[f, t, 2:18, 0:4, :] = jnp.zeros((16, 4, 128), f32)
            e[f, t, 2:18, 20:32, :] = jnp.zeros((16, 12, 128), f32)

    for load in loads:
        load.wait()
    for i, z in ((0, 14), (1, 0)):
        zs[i, 0] = f_v[z : z + 2].astype(f32)
        zs[i, 1] = w_v[z : z + 2]
        ys[i, 0] = f_v[:, z : z + 2, :].astype(f32)
        ys[i, 1] = w_v[:, z : z + 2, :]
    for i, (dz, dy) in enumerate(DIRS[4:]):
        z, y = (15 if dz > 0 else 0), (15 if dy > 0 else 0)
        ds[i, 0:1] = f_v[z, y : y + 1, :].astype(f32)
        ds[i, 1:2] = w_v[z, y : y + 1, :]
    for t in range(2):
        e[0, t, 2:18, 4:20, :] = f_v[:, :, 128 * t : 128 * t + 128].astype(f32)
        e[1, t, 2:18, 4:20, :] = w_v[:, :, 128 * t : 128 * t + 128]

    pl.semaphore_wait(barrier, count)

    def copy(source, target, slot, off):
        return pltpu.make_async_remote_copy(
            src_ref=source, dst_ref=target, send_sem=send_sem.at[slot], recv_sem=recv_sem.at[slot],
            device_id=device(off), device_id_type=MESH)

    def start(messages):
        for source, target, slot, off, fill in messages:
            @pl.when(has(off))
            def _(source=source, target=target, slot=slot, off=off):
                copy(source, target, slot, off).start()

    def receive(messages):
        for source, target, slot, off, fill in messages:
            there = has(negative(off))

            @pl.when(there)
            def _(source=source, target=target, slot=slot, off=off):
                copy(source, target, slot, off).wait_recv()

            @pl.when(jnp.logical_not(there))
            def _(target=target, fill=fill):
                fill(target)

    def sent(messages):
        for source, target, slot, off, fill in messages:
            @pl.when(has(off))
            def _(source=source, target=target, slot=slot, off=off):
                copy(source, target, slot, off).wait_send()

    def fill_pair(target):
        shape = target.shape[1:]
        target[0] = jnp.full(shape, OUTSIDE, f32)
        target[1] = jnp.zeros(shape, f32)

    def fill_row(target):
        row = lax.broadcasted_iota(jnp.int32, (2, 256), 0)
        target[...] = jnp.where(row == 0, OUTSIDE, 0.0).astype(f32)

    def fill_coarse(target):
        shape = target.shape[1:]
        target[0] = jnp.zeros(shape, f32)
        target[1] = jnp.full(shape, OUTSIDE, f32)

    raw = []
    for slot, d in enumerate(DIRS):
        off = d + (0,)
        if slot < 2:
            raw.append((zs.at[slot], zr.at[slot], slot, off, fill_pair))
        elif slot < 4:
            raw.append((ys.at[slot - 2], yr.at[slot - 2], slot, off, fill_pair))
        else:
            raw.append((ds.at[slot - 4], dr.at[slot - 4], slot, off, fill_row))
    start(raw)

    on_top = jnp.where(me["slab"] == size["slab"] - 1, spot_power, 0.0).astype(f32)
    y0, x0 = me["grp"] * 16 - 4, me["brick"] * 256

    def laser(substep, t, r, n):
        lane = lane_of(n)
        y = lax.broadcasted_iota(jnp.int32, (n, 128), 0) + (y0 + r)
        x = x0 + (jnp.where(lane < 64, lane + 224, lane - 96) if t == 2 else lane + 128 * t)
        total = jnp.zeros((n, 128), f32)
        for p in range(4):
            hit = (y == by_ref[substep, p]) & (x == bx_ref[substep, p])
            total = total + jnp.where(hit, on_top, 0.0)
        return total

    receive(raw)
    for t in range(2):
        cols = slice(128 * t, 128 * t + 128)
        for f in range(2):
            e[f, t, 0:2, 4:20, :] = zr[0, f, :, :, cols]
            e[f, t, 18:20, 4:20, :] = zr[1, f, :, :, cols]
            e[f, t, 2:18, 2:4, :] = yr[0, f, :, :, cols]
            e[f, t, 2:18, 20:22, :] = yr[1, f, :, :, cols]
            for i, (dz, dy) in enumerate(DIRS[4:]):
                z, y = (1 if dz > 0 else 18), (3 if dy > 0 else 20)
                e[f, t, z, y : y + 1, :] = dr[i, f : f + 1, cols]

    lane = lane_of(8)
    group = lane // 16
    for f in range(2):
        for v in range(8):
            right, left = jnp.zeros((8, 128), f32), jnp.zeros((8, 128), f32)
            for j in range(8):
                r = 8 * v + j
                if r < 60:
                    z, y = r // 3, 8 * (r % 3)
                    a, b = e[f, 1, z, y : y + 8, :], e[f, 0, z, y : y + 8, :]
                    right = jnp.where(group == j, pltpu.roll(a, (16 * j - 112) % 128, 1), right)
                    left = jnp.where(group == j, pltpu.roll(b, 16 * j, 1) if j else b, left)
            xs[0, f, v] = right
            xs[1, f, v] = left
    along = [(xs.at[i], xr.at[i], 8 + i, (0, 0, 1 - 2 * i), fill_pair) for i in range(2)]
    start(along)

    def raw_t(t, z, r, n):
        return e[1, t, z, r : r + n, :]

    def mid_t(t, z, r, n):
        return t1[t, z, r : r + n, :]

    def put_1(t, z, value):
        t1[t, z, 3:27, :] = value

    def put_2(t, z, value):
        t2[t, z - 2] = value

    def substeps(tiles):
        conductances(e, g, tiles)
        for_24 = functools.partial(raw_t, n=24)
        for_16 = functools.partial(mid_t, n=16)
        thermal(for_24, put_1, g, [laser(0, t, 3, 24) for t in tiles], tiles, 1, 19, 3, 24)
        thermal(for_16, put_2, g, [laser(1, t, 4, 16) for t in tiles], tiles, 2, 18, 4, 16)

    def coarsen(tiles, pick):
        for z in range(8):
            for t in tiles:
                fa, fb = e[0, t, 2 * z + 2, 4:20, :], e[0, t, 2 * z + 3, 4:20, :]
                qs[0, t, z] = fa * t2[t, 2 * z] + fb * t2[t, 2 * z + 1]
                qs[1, t, z] = fa + fb
        rows = []
        for f in range(2):
            pairs = [qs[f, t, :, pl.ds(0, 8, stride=2), :] + qs[f, t, :, pl.ds(1, 8, stride=2), :] for t in tiles]
            pairs = [p.reshape(64, 128) for p in pairs]
            rows.append((jnp.concatenate(pairs, axis=1) if len(pairs) > 1 else pairs[0]) * 0.125)
        q, solid = rows
        q1 = q.astype(bf16)
        rest = q - q1.astype(f32)
        q2 = rest.astype(bf16)
        q3 = (rest - q2.astype(f32)).astype(bf16)
        lhs = jnp.concatenate([q1, q2, q3, solid.astype(bf16)], axis=0)
        out = jnp.dot(lhs, pick[...], preferred_element_type=f32)
        return (out[0:64] + out[64:128]) + out[128:192], out[192:256]

    substeps((0, 1))
    for f, field in enumerate(coarsen((0, 1), pick_m)):
        cbm[f] = field.reshape(8, 8, 128)
    last6, first6 = cbm.at[:, 2:8], cbm.at[:, 0:6]
    swap = []
    for slot, d in enumerate(DIRS):
        off = d + (0,)
        if slot < 2:
            source, target = (last6, first6)[slot], czr.at[slot]
        elif slot < 4:
            source, target = cbm, cyr.at[slot - 2]
        else:
            source, target = (last6 if d[0] > 0 else first6), cdr.at[slot - 4]
        swap.append((source, target, 10 + slot, off, fill_coarse))
    start(swap)

    for f in range(2):
        for r in range(60):
            z, y = r // 3, 8 * (r % 3)
            a, b = e[f, 1, z, y : y + 8, :], e[f, 0, z, y : y + 8, :]
            e[f, 2, z, y : y + 8, :] = jnp.where(lane < 64, pltpu.roll(a, 32, 1), pltpu.roll(b, 96, 1))
        e[f, 2, :, 24:32, :] = jnp.zeros((20, 8, 128), f32)
    receive(along)
    for f in range(2):
        for r in range(60):
            v, j = r // 8, r % 8
            z, y = r // 3, 8 * (r % 3)
            before, after = xr[0, f, v], xr[1, f, v]
            before = pltpu.roll(before, (80 - 16 * j) % 128, 1) if (80 - 16 * j) % 128 else before
            after = pltpu.roll(after, (32 - 16 * j) % 128, 1) if (32 - 16 * j) % 128 else after
            own = jnp.where((lane >= 32) & (lane < 48), after, e[f, 2, z, y : y + 8, :])
            e[f, 2, z, y : y + 8, :] = jnp.where((lane >= 80) & (lane < 96), before, own)

    substeps((2,))
    for f, field in enumerate(coarsen((2,), pick_w)):
        field = field.reshape(8, 8, 128)
        packed = field[0]
        for z in range(1, 8):
            packed = jnp.where(group == z, field[z], packed)
        cbw[f] = packed
    swap_w = [(cbw, cwr.at[slot], 18 + slot, d + (0,), fill_coarse) for slot, d in enumerate(DIRS)]
    start(swap_w)

    lane16 = lane_of(16)
    for z in range(16):
        w = t2[2, z]
        t_v[z, :, 0:128] = jnp.where(lane16 < 16, pltpu.roll(w, 32, 1), t2[0, z])
        t_v[z, :, 128:256] = jnp.where(lane16 >= 112, pltpu.roll(w, 96, 1), t2[1, z])
    saves = [pltpu.make_async_copy(t_v, t_out, out_sem.at[0]), pltpu.make_async_copy(u_v, u_out, out_sem.at[1])]
    saves[0].start()

    def place(main, packed, first, planes, tile):
        for f in range(2):
            p = packed[f]
            for i, z in enumerate(planes):
                rows = slice(8 * tile, 8 * tile + 8)
                left, right = (122 - 16 * z) % 128, (120 - 16 * z) % 128
                a = pltpu.roll(p, left, 1) if left else p
                b = pltpu.roll(p, right, 1) if right else p
                cx[f, 0, first + i, rows, :] = jnp.where(lane == 0, a, jnp.where(lane == 127, b, main[f, i]))
                cx[f, 1, first + i, rows, :] = jnp.where(lane < 6, b, jnp.where(lane >= 122, a, 0.0))

    upper, lower = range(2, 8), range(0, 6)
    place(cbm, cbw, 6, range(8), 1)
    receive(swap)
    receive(swap_w)
    place(czr.at[0], cwr.at[0], 0, upper, 1)
    place(czr.at[1], cwr.at[1], 14, lower, 1)
    place(cyr.at[0], cwr.at[2], 6, range(8), 0)
    place(cyr.at[1], cwr.at[3], 6, range(8), 2)
    for i, (dz, dy) in enumerate(DIRS[4:]):
        place(cdr.at[i], cwr.at[4 + i], 0 if dz > 0 else 14, upper if dz > 0 else lower, 0 if dy > 0 else 2)

    sweeps(cx, u_v, dira, dirb, res, inv, spr, div)
    saves[1].start()
    for save in saves:
        save.wait()
    for messages in (raw, along, swap, swap_w):
        sent(messages)


def sweeps(cx, u, dira, dirb, res, inv, spr, div):
    centre_value = (eigen_high + eigen_low) / 2.0
    radius = (eigen_high - eigen_low) / 2.0
    sigma = centre_value / radius
    rho = 1.0 / sigma
    half = 0.5 * stress_factor
    both = (0, 1)

    for z in range(1, 19):
        s = [cx[0, t, z, 3:27, :] for t in both]
        ahead, behind = next_x(s), prev_x(s)
        for t in both:
            solid = cx[1, t, z, 3:27, :]
            spring = 0.5 + 1.5 * solid
            inverse = jnp.where(solid < -1.0, 0.0, 1.0 / (6.0 * shear_modulus + 2.0 * coupling + spring))
            inv[t, z, 3:27, :] = inverse
            spr[t, z, 3:27, :] = spring + 6.0 * shear_modulus
            scaled = inverse * (1.0 / centre_value)
            force = (
                half * (cx[0, t, z - 1, 3:27, :] - cx[0, t, z + 1, 3:27, :]),
                half * (cx[0, t, z, 2:26, :] - cx[0, t, z, 4:28, :]),
                half * (behind[t] - ahead[t]),
            )
            for d in range(3):
                res[d, t, z, 3:27, :] = force[d]
                dira[d, t, z, 3:27, :] = force[d] * scaled
    for d in range(3):
        u[d] = dira[d, 0, 6:14, 8:16, :]

    old, new = dira, dirb
    for sweep in range(SWEEPS - 1):
        halo = SWEEPS - 2 - sweep
        rho_next = 1.0 / (2.0 * sigma - rho)
        keep, gain = rho_next * rho, 2.0 * rho_next / radius
        first, last, r, n = 6 - halo, 14 + halo, 8 - halo, (16 if halo else 8)
        rows, m = slice(r, r + n), (24 if halo == 4 else 16)
        near = slice(r - 1, r - 1 + m)

        def spread(z):
            x = [old[2, t, z, near, :] for t in both]
            ahead = next_x(x)
            for t in both:
                dz = old[0, t, z + 1, near, :] - old[0, t, z, near, :]
                dy = old[1, t, z, r : r + m, :] - old[1, t, z, near, :]
                div[t, z, near, :] = dz + dy + (ahead[t] - x[t])

        spread(first - 1)
        for z in range(first, last):
            spread(z)
            here = [div[t, z, rows, :] for t in both]
            behind = prev_x(here)
            v = [[old[d, t, z, rows, :] for t in both] for d in range(3)]
            ahead_v, behind_v = [next_x(a) for a in v], [prev_x(a) for a in v]
            for t in both if halo else (0,):
                back = (
                    div[t, z - 1, rows, :] - here[t],
                    div[t, z, r - 1 : r + n - 1, :] - here[t],
                    behind[t] - here[t],
                )
                factor, inverse = spr[t, z, rows, :], inv[t, z, rows, :] * gain
                for d in range(3):
                    side = old[d, t, z, r + 1 : r + n + 1, :] + old[d, t, z, r - 1 : r + n - 1, :]
                    over = old[d, t, z + 1, rows, :] + old[d, t, z - 1, rows, :]
                    around = (ahead_v[d][t] + behind_v[d][t]) + side + over
                    left = res[d, t, z, rows, :] - (factor * v[d][t] - shear_modulus * around + coupling * back[d])
                    ahead_d = keep * v[d][t] + inverse * left
                    if halo:
                        res[d, t, z, rows, :] = left
                        new[d, t, z, rows, :] = ahead_d
                    if t == 0 and 6 <= z < 14:
                        u[d, z - 6] = u[d, z - 6] + ahead_d[8 - r : 16 - r]
        rho = rho_next
        old, new = new, old


def per_device(warmth, flag, north, east):
    vmem = pltpu.VMEM
    ext = lambda *s: vmem(s, f32)
    scratch = [
        ext(16, 16, 256), vmem((16, 16, 256), jnp.int32), pltpu.SMEM((2, 4), jnp.int32), pltpu.SMEM((2, 4), jnp.int32),
        ext(2, 3, 20, 32, 128), ext(4, 3, 20, 32, 128), ext(3, 20, 32, 128), ext(3, 16, 16, 128),
        ext(2, 2, 2, 16, 256), ext(2, 2, 2, 16, 256), ext(2, 2, 16, 2, 256), ext(2, 2, 16, 2, 256), ext(4, 2, 256), ext(4, 2, 256),
        ext(2, 2, 8, 8, 128), ext(2, 2, 8, 8, 128), ext(2, 3, 8, 16, 128),
        ext(2, 8, 8, 128), ext(2, 8, 128), ext(2, 2, 6, 8, 128), ext(2, 2, 8, 8, 128), ext(4, 2, 6, 8, 128), ext(8, 2, 8, 128),
        ext(2, 2, 20, 32, 128), ext(3, 2, 20, 32, 128), ext(3, 2, 20, 32, 128), ext(3, 2, 20, 32, 128),
        ext(2, 20, 32, 128), ext(2, 20, 32, 128), ext(2, 20, 32, 128),
        vmem((256, 128), bf16), vmem((128, 128), bf16), ext(16, 16, 256), ext(3, 8, 8, 128),
        pltpu.SemaphoreType.DMA((4,)), pltpu.SemaphoreType.DMA((26,)), pltpu.SemaphoreType.DMA((26,)), pltpu.SemaphoreType.DMA((2,)),
    ]
    anywhere = pl.BlockSpec(memory_space=pl.ANY)
    return pl.pallas_call(
        kernel,
        out_shape=(jax.ShapeDtypeStruct((16, 16, 256), f32), jax.ShapeDtypeStruct((3, 8, 8, 128), f32)),
        in_specs=[anywhere] * 4,
        out_specs=(anywhere, anywhere),
        scratch_shapes=scratch,
        compiler_params=pltpu.CompilerParams(collective_id=0, has_side_effects=True),
    )(warmth, flag, north, east)


def solution(mesh):
    in_specs = (P("slab", "grp", "brick"), P("slab", "grp", "brick"), P(), P())
    out_specs = (P("slab", "grp", "brick"), P(None, "slab", "grp", "brick"))
    return jax.shard_map(per_device, mesh=mesh, in_specs=in_specs, out_specs=out_specs, check_vma=False)
```

time: 57.6 us -> 36.7 us (0.64)
  the two profiles are of different devices: /device:TPU:2 before, /device:TPU:487 now
where the time goes in v2:
time: 36.7 us; the launch traced here: 36.5 us
  Pallas kernels  33.6 us (92%)
  local copies, waits for them, and re-layouts  2.35 us (6%)
  between operations  0.65 us (2%)
    pallas_call x1, Pallas kernels, per_device(): pl.pallas_call(kernel, out_shape=(jax.ShapeDtypeStruct((16, 16, 256), f32...  33.6 us
    unnamed x4, local copies, waits for them, and re-layouts  2.35 us

profile of v2, /device:TPU:487, one launch (start us, length us, event | category | flops | bytes accessed | tf_op | source)
XLA Modules:
  0.0 36.5 jit_solution(12123411710682838683)
XLA Ops:
  0.6 33.6 %shard_map.59 = (f32[16,16,256]{2,1,0:T(8,128)}, f32[3,8,8,128]{3,2,1,0:T(8,128)}) custom-call(f32[16,16,256]{2,1,0:T(8,128)} %w_hbm.1, s32[16,16,256]{2,1,0:T(8,128)} %f_hbm.1, s32[2,4]{1,0:T(2,128)} %by_hbm.1, s32[2,4]{1,0:T(2,128)} %bx_hbm.1), custom_call_target="tpu_custom_call" | custom-call | tf_op jit(solution)/shard_map/pallas_call | solution.py:457
  34.2 0.0 copy-start
  34.2 1.7 %copy.8 = f32[16,16,256]{2,1,0:T(8,128)} copy(f32[16,16,256]{2,1,0:T(8,128)} %get-tuple-element.4) | data formatting | bytes 524288
  35.9 0.0 copy-done
  35.9 0.6 %copy.9 = f32[3,8,8,128]{3,2,1,0:T(8,128)} copy(f32[3,8,8,128]{3,2,1,0:T(8,128)S(1)} %copy-done) | data formatting | bytes 196608
Async XLA Ops:
  34.2 1.7 %copy-start = (f32[3,8,8,128]{3,2,1,0:T(8,128)S(1)}, f32[3,8,8,128]{3,2,1,0:T(8,128)}, u32[]{:S(2)}) copy-start(f32[3,8,8,128]{3,2,1,0:T(8,128)} %get-tuple-element.5) | copy-start | bytes 294916

commit v3 on v2

--- a/solution.py
+++ b/solution.py
@@ -79,11 +79,11 @@
             below[i] = fz
 
 
-def kernel(w_hbm, f_hbm, by_hbm, bx_hbm, t_out, u_out,
+def kernel(w_hbm, f_hbm, by_hbm, bx_hbm, t_v, u_v,
            w_v, f_v, by_ref, bx_ref, e, g, t1, t2,
            zs, zr, ys, yr, ds, dr, xs, xr, qs, cbm, cbw, czr, cyr, cdr, cwr,
-           cx, dira, dirb, res, inv, spr, div, pick_m, pick_w, t_v, u_v,
-           load_sem, send_sem, recv_sem, out_sem):
+           cx, dira, dirb, res, inv, spr, div, pick_m, pick_w,
+           load_sem, send_sem, recv_sem):
     me = {a: lax.axis_index(a) for a in ("slab", "grp", "brick")}
     size = {a: lax.axis_size(a) for a in ("slab", "grp", "brick")}
 
@@ -331,8 +331,6 @@
         w = t2[2, z]
         t_v[z, :, 0:128] = jnp.where(lane16 < 16, pltpu.roll(w, 32, 1), t2[0, z])
         t_v[z, :, 128:256] = jnp.where(lane16 >= 112, pltpu.roll(w, 96, 1), t2[1, z])
-    saves = [pltpu.make_async_copy(t_v, t_out, out_sem.at[0]), pltpu.make_async_copy(u_v, u_out, out_sem.at[1])]
-    saves[0].start()
 
     def place(main, packed, first, planes, tile):
         for f in range(2):
@@ -357,9 +355,6 @@
         place(cdr.at[i], cwr.at[4 + i], 0 if dz > 0 else 14, upper if dz > 0 else lower, 0 if dy > 0 else 2)
 
     sweeps(cx, u_v, dira, dirb, res, inv, spr, div)
-    saves[1].start()
-    for save in saves:
-        save.wait()
     for messages in (raw, along, swap, swap_w):
         sent(messages)
 
@@ -450,18 +445,36 @@
         ext(2, 8, 8, 128), ext(2, 8, 128), ext(2, 2, 6, 8, 128), ext(2, 2, 8, 8, 128), ext(4, 2, 6, 8, 128), ext(8, 2, 8, 128),
         ext(2, 2, 20, 32, 128), ext(3, 2, 20, 32, 128), ext(3, 2, 20, 32, 128), ext(3, 2, 20, 32, 128),
         ext(2, 20, 32, 128), ext(2, 20, 32, 128), ext(2, 20, 32, 128),
-        vmem((256, 128), bf16), vmem((128, 128), bf16), ext(16, 16, 256), ext(3, 8, 8, 128),
-        pltpu.SemaphoreType.DMA((4,)), pltpu.SemaphoreType.DMA((26,)), pltpu.SemaphoreType.DMA((26,)), pltpu.SemaphoreType.DMA((2,)),
+        vmem((256, 128), bf16), vmem((128, 128), bf16),
+        pltpu.SemaphoreType.DMA((4,)), pltpu.SemaphoreType.DMA((26,)), pltpu.SemaphoreType.DMA((26,)),
     ]
     anywhere = pl.BlockSpec(memory_space=pl.ANY)
+    local = pl.BlockSpec(memory_space=pltpu.VMEM)
+    shapes = (jax.ShapeDtypeStruct((16, 16, 256), f32), jax.ShapeDtypeStruct((3, 8, 8, 128), f32))
+    results = pl.pallas_call(
+        kernel,
+        out_shape=shapes,
+        in_specs=[pl.BlockSpec(memory_space=pltpu.HBM)] * 4,
+        out_specs=(local, local),
+        scratch_shapes=scratch,
+        compiler_params=pltpu.CompilerParams(collective_id=0, has_side_effects=True, vmem_limit_bytes=56098816),
+    )(warmth, flag, north, east)
     return pl.pallas_call(
-        kernel,
-        out_shape=(jax.ShapeDtypeStruct((16, 16, 256), f32), jax.ShapeDtypeStruct((3, 8, 8, 128), f32)),
-        in_specs=[anywhere] * 4,
+        store,
+        out_shape=shapes,
+        in_specs=[local, local],
         out_specs=(anywhere, anywhere),
-        scratch_shapes=scratch,
-        compiler_params=pltpu.CompilerParams(collective_id=0, has_side_effects=True),
-    )(warmth, flag, north, east)
+        scratch_shapes=[pltpu.SemaphoreType.DMA((2,))],
+        compiler_params=pltpu.CompilerParams(vmem_limit_bytes=4 * 2**20),
+    )(*results)
+
+
+def store(t, u, t_out, u_out, sem):
+    copies = [pltpu.make_async_copy(t, t_out, sem.at[0]), pltpu.make_async_copy(u, u_out, sem.at[1])]
+    for copy in copies:
+        copy.start()
+    for copy in copies:
+        copy.wait()
 
 
 def solution(mesh):

time: 36.7 us -> 35.9 us (0.978)
  local copies, waits for them, and re-layouts: 2.35 us -> 1.35 us
    unnamed x4, local copies, waits for them, and re-layouts: 2.35 us -> 1.35 us
    pallas_call x1 -> x2, Pallas kernels: 33.6 us -> 33.7 us  [the longest x1 32.9 us: per_device(): pl.pallas_call(kernel, out_shape=shapes, in_specs=[pl.BlockSpec(memory_sp...]
where the time goes in v3:
time: 35.9 us; the launch traced here: 35.7 us
  Pallas kernels  33.7 us (94%)
  local copies, waits for them, and re-layouts  1.35 us (4%)
  between operations  0.65 us (2%)
    pallas_call x1, Pallas kernels, per_device(): pl.pallas_call(kernel, out_shape=shapes, in_specs=[pl.BlockSpec(memory_sp...  32.9 us
    unnamed x4, local copies, waits for them, and re-layouts  1.35 us
    pallas_call x1, Pallas kernels, per_device(): pl.pallas_call(store, out_shape=shapes, in_specs=[local, local], out_spec...  0.75 us

profile of v3, /device:TPU:487, one launch (start us, length us, event | category | flops | bytes accessed | tf_op | source)
XLA Modules:
  0.0 35.7 jit_solution(8316210818143784232)
XLA Ops:
  0.6 0.0 copy-start
  0.6 0.7 %copy-done = s32[2,4]{1,0:T(2,128)S(1)} copy-done((s32[2,4]{1,0:T(2,128)S(1)}, s32[2,4]{1,0:T(2,128)}, u32[]{:S(2)}) %copy-start) | copy-done | bytes 56
  1.3 0.0 copy-start.1
  1.3 0.7 %copy-done.1 = s32[2,4]{1,0:T(2,128)S(1)} copy-done((s32[2,4]{1,0:T(2,128)S(1)}, s32[2,4]{1,0:T(2,128)}, u32[]{:S(2)}) %copy-start.1) | copy-done | bytes 56
  2.0 32.9 %shard_map.59 = (f32[16,16,256]{2,1,0:T(8,128)S(1)}, f32[3,8,8,128]{3,2,1,0:T(8,128)S(1)}) custom-call(f32[16,16,256]{2,1,0:T(8,128)} %w_hbm.1, s32[16,16,256]{2,1,0:T(8,128)} %f_hbm.1, s32[2,4]{1,0:T(2,128)S(1)} %copy-done, s32[2,4]{1,0:T(2,128)S(1)} %copy-done.1), custom_call_target="tpu_custom_call" | custom-call | tf_op jit(solution)/shard_map/pallas_call | solution.py:454
  34.9 0.7 %shard_map.60 = (f32[16,16,256]{2,1,0:T(8,128)}, f32[3,8,8,128]{3,2,1,0:T(8,128)}) custom-call(f32[16,16,256]{2,1,0:T(8,128)S(1)} %get-tuple-element.4.t, f32[3,8,8,128]{3,2,1,0:T(8,128)S(1)} %get-tuple-element.5.u), custom_call_target="tpu_custom_call" | custom-call | tf_op jit(solution)/shard_map/pallas_call | solution.py:462
Async XLA Ops:
  0.6 0.7 %copy-start = (s32[2,4]{1,0:T(2,128)S(1)}, s32[2,4]{1,0:T(2,128)}, u32[]{:S(2)}) copy-start(s32[2,4]{1,0:T(2,128)} %by_hbm.1) | copy-start | bytes 100
  1.3 0.7 %copy-start.1 = (s32[2,4]{1,0:T(2,128)S(1)}, s32[2,4]{1,0:T(2,128)}, u32[]{:S(2)}) copy-start(s32[2,4]{1,0:T(2,128)} %bx_hbm.1) | copy-start | bytes 100
